TPU v7x, 512 devices: a whole 4x8x8 slice. The times are simulated.
512 devices in a mesh: blk: 32 (over x, y_lo, core), fsdp: 16 (over z, y_hi).
Axes of the slice: x: 4, y: 8 (y_hi: 2, y_lo: 4; y = y_hi * 4 + y_lo), z: 8, core: 2. Of those that a mesh axis runs over, the one named last changes fastest.
Arguments:
- decoder_states: bfloat16 [8192, 4096], P('blk', 'fsdp'), may hold values from -10 to 10
- w_query: bfloat16 [4096, 4096], P('blk', 'fsdp'), may hold values from -0.09375 to 0.09375
- w_out_t: bfloat16 [4096, 4096], P('blk', 'fsdp'), may hold values from -0.1875 to 0.1875
- enc_keys: bfloat16 [8192, 4096], P('blk', 'fsdp'), may hold values from -80 to 80
- enc_values: bfloat16 [8192, 4096], P('blk', 'fsdp'), may hold values from -6 to 6
Outputs:
- attended: bfloat16 [8192, 4096], P(('blk', 'fsdp'))
All inputs are finite; a program needn't handle non-finite values.
Results may differ from a plain program's by a relative error of at most 0.0095.
Values may be sent and summed in bfloat16 or wider, within the bound.
A program may use at most 128 MiB of HBM per device.

v0:
```python
import math
import jax
import jax.numpy as jnp
from jax import lax
from jax.sharding import PartitionSpec as P

HEAD_DIM = 64


def absorb(fold_state, query_heads, key_rows, value_rows):
    running_top, running_sum, weighted = fold_state
    local_heads = query_heads.shape[1]
    key_heads = key_rows.reshape(key_rows.shape[0], local_heads, HEAD_DIM)
    value_heads = value_rows.reshape(value_rows.shape[0], local_heads, HEAD_DIM)
    scores = jnp.einsum(
        "qhd,khd->hqk", query_heads, key_heads, preferred_element_type=jnp.float32
    ) * (1.0 / math.sqrt(HEAD_DIM))
    new_top = jnp.max(scores, axis=2)
    rescale = jnp.exp(running_top - new_top)
    probability = jnp.exp(scores - new_top[:, :, None])
    running_sum = running_sum * rescale + jnp.sum(probability, axis=2)
    weighted = weighted * rescale[:, :, None] + jnp.einsum(
        "hqk,khd->hqd",
        probability.astype(jnp.bfloat16),
        value_heads,
        preferred_element_type=jnp.float32,
    )
    return (new_top, running_sum, weighted)


def shards(decoder_states, w_query, w_out_t, enc_keys, enc_values):
    query_full = lax.all_gather(w_query, "blk", axis=0, tiled=True)
    row_count = decoder_states.shape[0]
    columns = query_full.shape[1]
    local_heads = columns // HEAD_DIM
    queries = jnp.dot(
        lax.all_gather(decoder_states, "fsdp", axis=1, tiled=True),
        query_full,
        preferred_element_type=jnp.float32,
    ).astype(jnp.bfloat16)
    start_state = (
        jnp.full((local_heads, row_count), -jnp.inf, jnp.float32),
        jnp.zeros((local_heads, row_count), jnp.float32),
        jnp.zeros((local_heads, row_count, HEAD_DIM), jnp.float32),
    )
    query_heads = queries.reshape(row_count, local_heads, HEAD_DIM)
    final_state = absorb(
        start_state,
        query_heads,
        lax.all_gather(enc_keys, "blk", axis=0, tiled=True),
        lax.all_gather(enc_values, "blk", axis=0, tiled=True),
    )
    context = final_state[2] / final_state[1][:, :, None]
    context = jnp.transpose(context, (1, 0, 2)).reshape(row_count, columns).astype(jnp.bfloat16)
    out_full = lax.all_gather(w_out_t, "blk", axis=0, tiled=True)
    return lax.psum_scatter(
        lax.dot_general(
            context, out_full, (((1,), (1,)), ((), ())), preferred_element_type=jnp.float32
        ),
        "fsdp",
        scatter_dimension=0,
        tiled=True,
    ).astype(jnp.bfloat16)


def solution(mesh):
    in_specs = (
        P("blk", "fsdp"),
        P("blk", "fsdp"),
        P("blk", "fsdp"),
        P("blk", "fsdp"),
        P("blk", "fsdp"),
    )
    out_specs = P(("blk", "fsdp"), None)
    return jax.shard_map(shards, mesh=mesh, in_specs=in_specs, out_specs=out_specs, check_vma=False)
```

profile of v0, /device:TPU:8, one launch (start us, length us, event | category | flops | bytes accessed | tf_op | source)
XLA Modules:
  0.0 624.3 jit_solution(10942586508582458863)
XLA Ops:
  6.5 0.7 all-gather.6.cloned.1.call-update
  7.3 0.0 all-gather.8.cloned.1.call-start
  7.3 0.7 all-gather.8.cloned.1.call-update
  8.0 0.0 all-gather.10.cloned.1.call-start
  8.1 0.7 all-gather.10.cloned.1.call-update
  8.7 0.0 all-gather.12.cloned.1.call-start
  8.8 0.5 all-gather.12.cloned.1.call-update
  9.3 0.0 all-gather.14.cloned.1.call-start
  9.4 0.5 all-gather.14.cloned.1.call-update
  9.9 0.0 reduce-scatter.2.cloned.1.call-start
  10.0 110.0 %all-gather.6.cloned.1.call-done = bf16[256,4096]{1,0:T(8,128)(2,1)} async-done(((bf16[256,256]{1,0:T(8,128)(2,1)}), bf16[256,4096]{1,0:T(8,128)(2,1)}) %all-gather.6.cloned.1.call-update) | async-done | bytes 2097168 | tf_op jit(solution)/shard_map/all_gather | solution.py:37
  120.0 59.1 %all-gather.8.cloned.1.call-done = bf16[4096,256]{1,0:T(8,128)(2,1)} async-done(((bf16[128,256]{1,0:T(8,128)(2,1)}), bf16[4096,256]{1,0:T(8,128)(2,1)}) %all-gather.8.cloned.1.call-update) | async-done | bytes 2097168 | tf_op jit(solution)/shard_map/all_gather | solution.py:32
  179.0 3.1 convolution_convert_fusion
  182.2 63.7 %all-gather.10.cloned.1.call-done = bf16[8192,256]{1,0:T(8,128)(2,1)} async-done(((bf16[256,256]{1,0:T(8,128)(2,1)}), bf16[8192,256]{1,0:T(8,128)(2,1)}) %all-gather.10.cloned.1.call-update) | async-done | bytes 4194320 | tf_op jit(solution)/shard_map/all_gather | solution.py:50
  245.9 6.4 %copy.6 = bf16[8192,256]{0,1:T(8,128)(2,1)} copy(bf16[8192,256]{1,0:T(8,128)(2,1)} %all-gather.10.cloned.1.call-done) | data formatting | bytes 8388608 | tf_op jit(solution)/shard_map/all_gather | solution.py:50
  252.3 15.5 %multiply_reduce_fusion = (f32[4,256]{1,0:T(4,128)S(1)}, f32[4,256,8192]{2,1,0:T(8,128)}) fusion(bf16[256,4,64]{0,2,1:T(8,128)(2,1)S(1)} %bitcast.27, bf16[8192,4,64]{0,2,1:T(8,128)(2,1)} %bitcast.26), kind=kOutput, calls=%fused_computation.1 | convolution fusion | flops 1090518016 | bytes 37883904 | tf_op jit(solution)/shard_map/qhd,khd->hqk/dot_general | solution.py:15
  267.8 44.6 %all-gather.12.cloned.1.call-done = bf16[8192,256]{1,0:T(8,128)(2,1)} async-done(((bf16[256,256]{1,0:T(8,128)(2,1)}), bf16[8192,256]{1,0:T(8,128)(2,1)}) %all-gather.12.cloned.1.call-update) | async-done | bytes 4194320 | tf_op jit(solution)/shard_map/all_gather | solution.py:51
  312.4 6.4 %copy.7 = bf16[8192,256]{0,1:T(8,128)(2,1)} copy(bf16[8192,256]{1,0:T(8,128)(2,1)} %all-gather.12.cloned.1.call-done) | data formatting | bytes 8388608 | tf_op jit(solution)/shard_map/all_gather | solution.py:51
  318.8 14.1 %fusion = f32[4,256]{1,0:T(4,128)S(1)} fusion(f32[4,256,8192]{2,1,0:T(8,128)} %get-tuple-element.6, f32[4,256]{1,0:T(4,128)S(1)} %get-tuple-element.5), kind=kLoop, calls=%fused_computation.2 | loop fusion | flops 25164800 | bytes 33562624 | tf_op jit(solution)/shard_map/reduce_sum | solution.py:21
  332.9 15.5 %fusion.13 = bf16[256,4,64]{0,2,1:T(8,128)(2,1)S(1)} fusion(bf16[8192,4,64]{0,2,1:T(8,128)(2,1)} %bitcast.25, f32[4,256,8192]{2,1,0:T(8,128)} %get-tuple-element.6, f32[4,256]{1,0:T(4,128)S(1)} %get-tuple-element.5, f32[256,4]{0,1:T(4,128)S(1)} %bitcast_add_fusion, f32[256,4]{0,1:T(4,128)S(1)} %multiply_bitcast_fusion), kind=kOutput, calls=%fused_computation.9 | convolution fusion | flops 1099104256 | bytes 37892096 | tf_op jit(solution)/shard_map/hqk,khd->hqd/dot_general | solution.py:22
  348.5 27.8 %all-gather.14.cloned.1.call-done = bf16[4096,256]{1,0:T(8,128)(2,1)} async-done(((bf16[128,256]{1,0:T(8,128)(2,1)}), bf16[4096,256]{1,0:T(8,128)(2,1)}) %all-gather.14.cloned.1.call-update) | async-done | bytes 2097168 | tf_op jit(solution)/shard_map/all_gather | solution.py:55
  376.3 4.3 fusion.17
  380.6 235.3 %reduce-scatter.2.cloned.1.call-done = f32[16,4096]{1,0:T(8,128)} async-done(((f32[256,4096]{1,0:T(8,128)}), f32[16,4096]{1,0:T(8,128)}) %reduce-scatter.2.cloned.1.call-update) | async-done | bytes 262160 | tf_op jit(solution)/shard_map/reduce_scatter | solution.py:56
  615.8 1.6 convert_element_type.19
  (4 shorter events, 0.0 us)
Async XLA Ops:
  6.5 113.4 %all-gather.6.cloned.1.call-start = ((), (), s32[]{:S(2)}) async-start(), calls=%async_computation.1 | async-start | bytes 2228224 | tf_op jit(solution)/shard_map/all_gather | solution.py:37
  7.3 171.8 %all-gather.8.cloned.1.call-start = ((), (), s32[]{:S(2)}) async-start(), calls=%async_computation.2 | async-start | bytes 2162688 | tf_op jit(solution)/shard_map/all_gather | solution.py:32
  8.0 237.8 %all-gather.10.cloned.1.call-start = ((), (), s32[]{:S(2)}) async-start(), calls=%async_computation.3 | async-start | bytes 4325376 | tf_op jit(solution)/shard_map/all_gather | solution.py:50
  8.7 303.7 %all-gather.12.cloned.1.call-start = ((), (), s32[]{:S(2)}) async-start(), calls=%async_computation.4 | async-start | bytes 4325376 | tf_op jit(solution)/shard_map/all_gather | solution.py:51
  9.3 366.9 %all-gather.14.cloned.1.call-start = ((), (), s32[]{:S(2)}) async-start(), calls=%async_computation.5 | async-start | bytes 2162688 | tf_op jit(solution)/shard_map/all_gather | solution.py:55
  9.9 605.9 %reduce-scatter.2.cloned.1.call-start = ((), (), s32[]{:S(2)}) async-start(), calls=%async_computation.6 | async-start | bytes 4456448 | tf_op jit(solution)/shard_map/reduce_scatter | solution.py:56
Sparse Core Ops, SparseCore 0:
  10.4 109.5 all-gather.5
  122.1 56.8 all-gather.7
  181.2 64.6 all-gather.9
  247.9 64.5 all-gather.11
  314.4 61.7 all-gather.13
  380.7 235.0 reduce-scatter.1
where the time goes:
time: 625 us; the launch traced here: 624 us
  waiting for transfers between devices  544 us (87%)
  matrix products  38.5 us (6%)
  other arithmetic  15.7 us (3%)
  between operations  13.5 us (2%)
  local copies, waits for them, and re-layouts  12.8 us (2%)
    reduce_scatter x1, waiting for transfers between devices, shards(): lax.psum_scatter(lax.dot_general(context, out_full, (((1,), (1,)), ((), (...  235 us
    all_gather x1, waiting for transfers between devices, shards(): lax.all_gather(decoder_states, 'fsdp', axis=1, tiled=True)  110 us
    all_gather x1, waiting for transfers between devices, shards(): lax.all_gather(enc_keys, 'blk', axis=0, tiled=True)  63.7 us
    all_gather x1, waiting for transfers between devices, shards(): query_full = lax.all_gather(w_query, 'blk', axis=0, tiled=True)  59.1 us
    all_gather x1, waiting for transfers between devices, shards(): lax.all_gather(enc_values, 'blk', axis=0, tiled=True)  44.6 us
    all_gather x1, waiting for transfers between devices, shards(): out_full = lax.all_gather(w_out_t, 'blk', axis=0, tiled=True)  27.8 us
    dot_general x1, matrix products, absorb(): jnp.einsum('hqk,khd->hqd', probability.astype(jnp.bfloat16), value_heads,...  15.5 us
    dot_general x1, matrix products, absorb(): jnp.einsum('qhd,khd->hqk', query_heads, key_heads, preferred_element_type...  15.5 us
  transfers between devices with their start and end apart: 6, of which 6 were waited for; matrix products, arithmetic and copies ran while one was open for 10% of the time, Pallas kernels for 0%

commit v1 on v0

--- a/solution.py
+++ b/solution.py
@@ -29,7 +29,10 @@
 
 
 def shards(decoder_states, w_query, w_out_t, enc_keys, enc_values):
-    query_full = lax.all_gather(w_query, "blk", axis=0, tiled=True)
+    n_dev = lax.axis_size("blk")
+    blocks = jnp.stack([w_query for _ in range(n_dev)])
+    blocks = lax.all_to_all(blocks, "blk", split_axis=0, concat_axis=0)
+    query_full = jnp.concatenate(blocks, axis=0)
     row_count = decoder_states.shape[0]
     columns = query_full.shape[1]
     local_heads = columns // HEAD_DIM

time: 625 us -> 570 us (0.912)
  waiting for transfers between devices: 544 us -> 477 us
  starting transfers between devices: 0.19 us -> 9.65 us
    all_gather x1 -> x0, waiting for transfers between devices: 59.1 us -> none  [shards(): query_full = lax.all_gather(w_query, 'blk', axis=0, tiled=True)]
    all_to_all x0 -> x1, starting transfers between devices: none -> 9.49 us  [shards(): blocks = lax.all_to_all(blocks, 'blk', split_axis=0, concat_axis=0)]
  transfers between devices with their start and end apart: 6 -> 6, of which waited for: 6 -> 5; matrix products, arithmetic and copies ran while one was open for 10% -> 11% of each run, Pallas kernels for 0% -> 0%
where the time goes in v1:
time: 570 us; the launch traced here: 569 us
  waiting for transfers between devices  477 us (84%)
  matrix products  37.9 us (7%)
  other arithmetic  15.7 us (3%)
  local copies, waits for them, and re-layouts  15.2 us (3%)
  between operations  13.2 us (2%)
  starting transfers between devices  9.65 us (2%)
    reduce_scatter x1, waiting for transfers between devices, shards(): lax.psum_scatter(lax.dot_general(context, out_full, (((1,), (1,)), ((), (...  239 us
    all_gather x1, waiting for transfers between devices, shards(): lax.all_gather(decoder_states, 'fsdp', axis=1, tiled=True)  104 us
    all_gather x1, waiting for transfers between devices, shards(): lax.all_gather(enc_keys, 'blk', axis=0, tiled=True)  59.3 us
    all_gather x1, waiting for transfers between devices, shards(): lax.all_gather(enc_values, 'blk', axis=0, tiled=True)  44.8 us
    all_gather x1, waiting for transfers between devices, shards(): out_full = lax.all_gather(w_out_t, 'blk', axis=0, tiled=True)  27.8 us
    dot_general x1, matrix products, absorb(): jnp.einsum('qhd,khd->hqk', query_heads, key_heads, preferred_element_type...  15.6 us
    dot_general x1, matrix products, absorb(): jnp.einsum('hqk,khd->hqd', probability.astype(jnp.bfloat16), value_heads,...  15.5 us
    reduce_sum x1, other arithmetic, absorb(): running_sum = running_sum * rescale + jnp.sum(probability, axis=2)  14.1 us
  transfers between devices with their start and end apart: 6, of which 5 were waited for; matrix products, arithmetic and copies ran while one was open for 11% of the time, Pallas kernels for 0%

profile of v1, /device:TPU:8, one launch (start us, length us, event | category | flops | bytes accessed | tf_op | source)
XLA Modules:
  0.0 569.0 jit_solution(4697451843141418027)
XLA Ops:
  6.5 0.7 all-gather.5.cloned.1.call-update
  7.3 0.0 all-gather.7.cloned.1.call-start
  7.3 0.7 all-gather.7.cloned.1.call-update
  8.0 0.0 all-gather.9.cloned.1.call-start
  8.1 0.7 all-gather.9.cloned.1.call-update
  8.7 2.4 stack.2
  11.1 9.5 %all-to-all-start = ((bf16[32,128,256]{2,1,0:T(8,128)(2,1)}), bf16[32,128,256]{2,1,0:T(8,128)(2,1)S(1)}, u32[]{:S(2)}, u32[]{:S(2)}) async-start(bf16[32,128,256]{2,1,0:T(8,128)(2,1)} %stack.2), calls=%async_computation | async-start | bytes 4194304 | tf_op jit(solution)/shard_map/all_to_all | solution.py:34
  20.6 0.0 all-gather.11.cloned.1.call-start
  20.7 0.5 all-gather.11.cloned.1.call-update
  21.2 0.0 reduce-scatter.2.cloned.1.call-start
  21.3 103.9 %all-gather.5.cloned.1.call-done = bf16[256,4096]{1,0:T(8,128)(2,1)} async-done(((bf16[256,256]{1,0:T(8,128)(2,1)}), bf16[256,4096]{1,0:T(8,128)(2,1)}) %all-gather.5.cloned.1.call-update) | async-done | bytes 2097168 | tf_op jit(solution)/shard_map/all_gather | solution.py:40
  125.2 2.5 convolution_convert_fusion
  127.7 59.3 %all-gather.7.cloned.1.call-done = bf16[8192,256]{1,0:T(8,128)(2,1)} async-done(((bf16[256,256]{1,0:T(8,128)(2,1)}), bf16[8192,256]{1,0:T(8,128)(2,1)}) %all-gather.7.cloned.1.call-update) | async-done | bytes 4194320 | tf_op jit(solution)/shard_map/all_gather | solution.py:53
  187.0 6.4 %copy.6 = bf16[8192,256]{0,1:T(8,128)(2,1)} copy(bf16[8192,256]{1,0:T(8,128)(2,1)} %all-gather.7.cloned.1.call-done) | data formatting | bytes 8388608 | tf_op jit(solution)/shard_map/all_gather | solution.py:53
  193.4 15.6 %multiply_reduce_fusion = (f32[4,256]{1,0:T(4,128)S(1)}, f32[4,256,8192]{2,1,0:T(8,128)}) fusion(bf16[256,4,64]{0,2,1:T(8,128)(2,1)S(1)} %bitcast.29, bf16[8192,4,64]{0,2,1:T(8,128)(2,1)} %bitcast.27), kind=kOutput, calls=%fused_computation.1 | convolution fusion | flops 1090518016 | bytes 37883904 | tf_op jit(solution)/shard_map/qhd,khd->hqk/dot_general | solution.py:15
  209.0 44.8 %all-gather.9.cloned.1.call-done = bf16[8192,256]{1,0:T(8,128)(2,1)} async-done(((bf16[256,256]{1,0:T(8,128)(2,1)}), bf16[8192,256]{1,0:T(8,128)(2,1)}) %all-gather.9.cloned.1.call-update) | async-done | bytes 4194320 | tf_op jit(solution)/shard_map/all_gather | solution.py:54
  253.7 6.4 %copy.7 = bf16[8192,256]{0,1:T(8,128)(2,1)} copy(bf16[8192,256]{1,0:T(8,128)(2,1)} %all-gather.9.cloned.1.call-done) | data formatting | bytes 8388608 | tf_op jit(solution)/shard_map/all_gather | solution.py:54
  260.1 14.1 %fusion = f32[4,256]{1,0:T(4,128)S(1)} fusion(f32[4,256,8192]{2,1,0:T(8,128)} %get-tuple-element.6, f32[4,256]{1,0:T(4,128)S(1)} %get-tuple-element.5), kind=kLoop, calls=%fused_computation.2 | loop fusion | flops 25164800 | bytes 33562624 | tf_op jit(solution)/shard_map/reduce_sum | solution.py:21
  274.2 15.5 %fusion.13 = bf16[256,4,64]{0,2,1:T(8,128)(2,1)S(1)} fusion(bf16[8192,4,64]{0,2,1:T(8,128)(2,1)} %bitcast.26, f32[4,256,8192]{2,1,0:T(8,128)} %get-tuple-element.6, f32[4,256]{1,0:T(4,128)S(1)} %get-tuple-element.5, f32[256,4]{0,1:T(4,128)S(1)} %bitcast_add_fusion, f32[256,4]{0,1:T(4,128)S(1)} %multiply_bitcast_fusion), kind=kOutput, calls=%fused_computation.9 | convolution fusion | flops 1099104256 | bytes 37892096 | tf_op jit(solution)/shard_map/hqk,khd->hqd/dot_general | solution.py:22
  289.8 27.8 %all-gather.11.cloned.1.call-done = bf16[4096,256]{1,0:T(8,128)(2,1)} async-done(((bf16[128,256]{1,0:T(8,128)(2,1)}), bf16[4096,256]{1,0:T(8,128)(2,1)}) %all-gather.11.cloned.1.call-update) | async-done | bytes 2097168 | tf_op jit(solution)/shard_map/all_gather | solution.py:58
  317.6 4.3 fusion.17
  321.9 0.0 reduce-scatter.2.cloned.1.call-update
  321.9 239.0 %reduce-scatter.2.cloned.1.call-done = f32[16,4096]{1,0:T(8,128)} async-done(((f32[256,4096]{1,0:T(8,128)}), f32[16,4096]{1,0:T(8,128)}) %reduce-scatter.2.cloned.1.call-update) | async-done | bytes 262160 | tf_op jit(solution)/shard_map/reduce_scatter | solution.py:59
  560.8 1.6 convert_element_type.19
  (4 shorter events, 0.0 us)
Async XLA Ops:
  6.5 118.6 %all-gather.5.cloned.1.call-start = ((), (), s32[]{:S(2)}) async-start(), calls=%async_computation.2 | async-start | bytes 2228224 | tf_op jit(solution)/shard_map/all_gather | solution.py:40
  7.3 179.8 %all-gather.7.cloned.1.call-start = ((), (), s32[]{:S(2)}) async-start(), calls=%async_computation.3 | async-start | bytes 4325376 | tf_op jit(solution)/shard_map/all_gather | solution.py:53
  8.0 245.7 %all-gather.9.cloned.1.call-start = ((), (), s32[]{:S(2)}) async-start(), calls=%async_computation.4 | async-start | bytes 4325376 | tf_op jit(solution)/shard_map/all_gather | solution.py:54
  11.1 114.0 %all-to-all-start = ((bf16[32,128,256]{2,1,0:T(8,128)(2,1)}), bf16[32,128,256]{2,1,0:T(8,128)(2,1)S(1)}, u32[]{:S(2)}, u32[]{:S(2)}) async-start(bf16[32,128,256]{2,1,0:T(8,128)(2,1)} %stack.2), calls=%async_computation | async-start | bytes 4194304 | tf_op jit(solution)/shard_map/all_to_all | solution.py:34
  20.6 296.9 %all-gather.11.cloned.1.call-start = ((), (), s32[]{:S(2)}) async-start(), calls=%async_computation.5 | async-start | bytes 2162688 | tf_op jit(solution)/shard_map/all_gather | solution.py:58
  21.2 539.6 %reduce-scatter.2.cloned.1.call-start = ((), (), s32[]{:S(2)}) async-start(), calls=%async_computation.6 | async-start | bytes 4456448 | tf_op jit(solution)/shard_map/reduce_scatter | solution.py:59
Sparse Core Ops, SparseCore 0:
  10.4 114.6 all-gather.4
  127.3 59.6 all-gather.6
  189.2 64.5 all-gather.8
  255.8 61.7 all-gather.10
  322.0 238.7 reduce-scatter.1
